TPU v7x, 32 devices: a whole 2x2x4 slice. The times are simulated.
32 devices in a mesh: dp: 8 (over z, y), mp: 4 (over x, core).
Axes of the slice: x: 2, y: 2, z: 4, core: 2. Of those that a mesh axis runs over, the one named last changes fastest.
Arguments:
- activations: bfloat16 [4, 4096, 5120], P(None, 'dp'), may hold values from -60 to 60
- task_weights: bfloat16 [4, 5120, 512], P(None, 'dp', 'mp'), may hold values from -6 to 6
Outputs:
- merged: float32 [5120, 512], P('dp', 'mp')
All inputs are finite; a program needn't handle non-finite values.
Results may differ from a plain program's by a relative error of at most 0.0015.
Values may be sent and summed in bfloat16 or wider, within the bound.
A program may use at most 128 MiB of HBM per device.

v0:
```python
import jax
import jax.numpy as jnp
from jax import lax
from jax.sharding import PartitionSpec as P

ITERS = 2


ALPHA = 0.9


def column_sum(left, right):
    return jnp.sum(left * right, axis=0)


def shards(activations, task_weights):
    tasks, tokens, width = activations.shape
    n_rows = lax.axis_size("dp")
    total = tasks * tokens * n_rows
    full_weights = lax.all_gather(task_weights, "dp", axis=1, tiled=True)
    outputs = jnp.einsum(
        "tnk,tkc->tnc", activations, full_weights, preferred_element_type=jnp.float32
    ).astype(jnp.bfloat16)
    squares = jnp.einsum(
        "tnk,tnk->tk", activations, activations, preferred_element_type=jnp.float32
    )
    rows_x = activations
    cross = jnp.einsum("tnk,tnc->kc", rows_x, outputs, preferred_element_type=jnp.float32)
    w_rows = full_weights.astype(jnp.float32)
    diag_part = jnp.sum(squares[:, :, None] * w_rows, axis=0)
    target = lax.psum_scatter(
        (ALPHA * cross + (1.0 - ALPHA) * diag_part) / total, "dp", scatter_dimension=0, tiled=True
    )
    squares_all = jnp.sum(squares, axis=0)

    def apply(vector):
        full_vector = lax.all_gather(vector, "dp", axis=0, tiled=True)
        projected = jnp.stack(
            [
                jnp.dot(
                    activations[task].astype(jnp.float32),
                    full_vector,
                    precision=lax.Precision.HIGHEST,
                )
                for task in range(tasks)
            ],
            axis=0,
        )
        rows_x = activations.astype(jnp.float32)
        inner = jnp.einsum("tnk,tnc->kc", rows_x, projected, precision=lax.Precision.HIGHEST)
        return lax.psum_scatter(
            (ALPHA * inner + (1.0 - ALPHA) * squares_all[:, None] * full_vector) / total,
            "dp",
            scatter_dimension=0,
            tiled=True,
        )

    def norm_of(residual):
        return lax.psum(column_sum(residual, residual), "dp")

    merged = jnp.mean(task_weights.astype(jnp.float32), axis=0)
    residual = target - apply(merged)
    direction = residual
    norm_now = norm_of(residual)
    for step in range(ITERS):
        image = apply(direction)
        alpha = norm_now / lax.psum(column_sum(direction, image), "dp")
        merged = merged + alpha * direction
        if step + 1 < ITERS:
            residual = residual - alpha * image
            norm_next = norm_of(residual)
            direction = residual + norm_next / norm_now * direction
            norm_now = norm_next
    return merged


def solution(mesh):
    return jax.shard_map(
        shards,
        mesh=mesh,
        in_specs=(P(None, "dp", None), P(None, "dp", "mp")),
        out_specs=P("dp", "mp"),
        check_vma=False,
    )
```

profile of v0, /device:TPU:0, one launch (start us, length us, event | category | flops | bytes accessed | tf_op | source)
XLA Modules:
  0.0 708.9 jit_solution(16035127164551259275)
XLA Ops:
  6.5 0.0 all-gather.7.cloned.1.call-start
  6.5 1.2 convert_reduce_fusion
  7.7 0.2 copy.4
  7.9 0.8 broadcast_multiply_fusion
  8.7 0.0 all-gather.7.cloned.1.call-update
  8.7 0.0 all-gather.5.cloned.1.call-start
  8.7 0.7 all-gather.5.cloned.1.call-update
  9.4 0.0 reduce-scatter.7.cloned.1.call-start
  9.5 8.8 %fusion = f32[4,5120]{1,0:T(4,128)S(1)} fusion(bf16[4,512,5120]{2,1,0:T(8,128)(2,1)} %param.2), kind=kLoop, calls=%fused_computation.1 | loop fusion | flops 31436800 | bytes 21053440 | tf_op jit(solution)/shard_map/tnk,tnk->tk/dot_general | solution.py:24
  18.4 48.5 %all-gather.7.cloned.1.call-done = f32[5120,128]{0,1:T(8,128)} async-done(((f32[640,128]{0,1:T(8,128)}), f32[5120,128]{0,1:T(8,128)}) %all-gather.7.cloned.1.call-update) | async-done | bytes 2621456 | tf_op jit(solution)/shard_map/all_gather | solution.py:37
  66.9 0.0 copy-start
  66.9 8.6 %fusion.80 = f32[1,512,128]{1,2,0:T(8,128)S(1)} fusion(f32[5120,128]{0,1:T(8,128)} %all-gather.7.cloned.1.call-done, bf16[4,512,5120]{2,1,0:T(8,128)(2,1)} %param.2), kind=kOutput, calls=%fused_computation.70 | convolution fusion | flops 4026531840 | bytes 8126464 | tf_op jit(solution)/shard_map/dot_general | solution.py:40
  75.5 0.0 copy-done
  75.5 7.9 %fusion.71 = f32[1,512,128]{1,2,0:T(8,128)S(1)} fusion(f32[5120,128]{0,1:T(8,128)S(1)} %copy-done, bf16[4,512,5120]{2,1,0:T(8,128)(2,1)} %param.2), kind=kOutput, calls=%fused_computation.67 | convolution fusion | flops 4026531840 | bytes 8126464 | tf_op jit(solution)/shard_map/dot_general | solution.py:40
  83.5 7.7 %fusion.62 = f32[1,512,128]{1,2,0:T(8,128)S(1)} fusion(f32[5120,128]{0,1:T(8,128)S(1)} %copy-done, bf16[4,512,5120]{2,1,0:T(8,128)(2,1)} %param.2), kind=kOutput, calls=%fused_computation.64 | convolution fusion | flops 4026531840 | bytes 8126464 | tf_op jit(solution)/shard_map/dot_general | solution.py:40
  91.2 8.2 %fusion.53 = f32[1,512,128]{1,2,0:T(8,128)S(1)} fusion(f32[5120,128]{0,1:T(8,128)S(1)} %copy-done, bf16[4,512,5120]{2,1,0:T(8,128)(2,1)} %param.2), kind=kOutput, calls=%fused_computation.61 | convolution fusion | flops 4026531840 | bytes 8126464 | tf_op jit(solution)/shard_map/dot_general | solution.py:40
  99.4 13.8 %fusion.12 = f32[5120,128]{0,1:T(8,128)} fusion(bf16[4,512,5120]{2,1,0:T(8,128)(2,1)} %param.2, f32[5120,128]{0,1:T(8,128)S(1)} %copy-done, f32[5120]{0:T(1024)S(1)} %broadcast_multiply_fusion.1, f32[1,512,128]{1,2,0:T(8,128)S(1)} %fusion.80, f32[1,512,128]{1,2,0:T(8,128)S(1)} %fusion.71, f32[1,512,128]{1,2,0:T(8,128)S(1)} %fusion.62, ...), kind=kOutput, calls=%fused_computation.18 | convolution fusion | flops 16109535232 | bytes 27283456 | tf_op jit(solution)/shard_map/tnk,tnc->kc/dot_general | solution.py:50
  113.2 0.0 reduce-scatter.7.cloned.1.call-update
  113.2 0.0 reduce-scatter.5.cloned.1.call-start
  113.2 40.3 %all-gather.5.cloned.1.call-done = bf16[4,5120,128]{2,1,0:T(8,128)(2,1)} async-done(((bf16[4,640,128]{2,1,0:T(8,128)(2,1)}), bf16[4,5120,128]{2,1,0:T(8,128)(2,1)}) %all-gather.5.cloned.1.call-update) | async-done | bytes 5242896 | tf_op jit(solution)/shard_map/all_gather | solution.py:20
  153.5 10.7 %multiply_reduce_fusion = f32[5120,128]{1,0:T(8,128)} fusion(bf16[4,5120,128]{2,1,0:T(8,128)(2,1)} %all-gather.5.cloned.1.call-done, f32[4,5120]{1,0:T(4,128)S(1)} %fusion), kind=kLoop, calls=%fused_computation.2 | loop fusion | flops 7208960 | bytes 7946240 | tf_op jit(solution)/shard_map/reduce_sum | solution.py:30
  164.2 2.1 copy.5
  166.3 24.7 %fusion.10 = f32[5120,128]{0,1:T(8,128)} fusion(bf16[4,512,5120]{2,1,0:T(8,128)(2,1)} %param.2, f32[5120,128]{0,1:T(8,128)S(1)} %copy.5, bf16[4,5120,128]{2,1,0:T(8,128)(2,1)} %all-gather.5.cloned.1.call-done), kind=kOutput, calls=%fused_computation.16 | convolution fusion | flops 5371592704 | bytes 31457280 | tf_op jit(solution)/shard_map/tnk,tnc->kc/dot_general | solution.py:28
  191.0 0.0 reduce-scatter.5.cloned.1.call-update
  191.0 0.0 all-gather.9.cloned.1.call-start
  191.1 35.4 %reduce-scatter.7.cloned.1.call-done = f32[640,128]{0,1:T(8,128)} async-done(((f32[5120,128]{0,1:T(8,128)}), f32[640,128]{0,1:T(8,128)}) %reduce-scatter.7.cloned.1.call-update) | async-done | bytes 327696 | tf_op jit(solution)/shard_map/reduce_scatter | solution.py:51
  226.5 73.5 %reduce-scatter.5.cloned.1.call-done = f32[640,128]{0,1:T(8,128)} async-done(((f32[5120,128]{0,1:T(8,128)}), f32[640,128]{0,1:T(8,128)}) %reduce-scatter.5.cloned.1.call-update) | async-done | bytes 327696 | tf_op jit(solution)/shard_map/reduce_scatter | solution.py:31
  300.0 1.8 sub.6
  301.9 0.0 all-gather.9.cloned.1.call-update
  301.9 0.2 reduce-scatter.9.cloned.1.call-start
  302.1 53.7 %all-gather.9.cloned.1.call-done = f32[5120,128]{0,1:T(8,128)} async-done(((f32[640,128]{0,1:T(8,128)}), f32[5120,128]{0,1:T(8,128)}) %all-gather.9.cloned.1.call-update) | async-done | bytes 2621456 | tf_op jit(solution)/shard_map/all_gather | solution.py:37
  355.8 8.6 %fusion.83 = f32[1,512,128]{1,2,0:T(8,128)S(1)} fusion(f32[5120,128]{0,1:T(8,128)} %all-gather.9.cloned.1.call-done, bf16[4,512,5120]{2,1,0:T(8,128)(2,1)} %param.2), kind=kOutput, calls=%fused_computation.71 | convolution fusion | flops 4026531840 | bytes 8126464 | tf_op jit(solution)/shard_map/dot_general | solution.py:40
  364.5 0.0 copy-done.2
  364.5 7.7 %fusion.74 = f32[1,512,128]{1,2,0:T(8,128)S(1)} fusion(f32[5120,128]{0,1:T(8,128)S(1)} %copy-done.2, bf16[4,512,5120]{2,1,0:T(8,128)(2,1)} %param.2), kind=kOutput, calls=%fused_computation.68 | convolution fusion | flops 4026531840 | bytes 8126464 | tf_op jit(solution)/shard_map/dot_general | solution.py:40
  372.2 7.7 %fusion.65 = f32[1,512,128]{1,2,0:T(8,128)S(1)} fusion(f32[5120,128]{0,1:T(8,128)S(1)} %copy-done.2, bf16[4,512,5120]{2,1,0:T(8,128)(2,1)} %param.2), kind=kOutput, calls=%fused_computation.65 | convolution fusion | flops 4026531840 | bytes 8126464 | tf_op jit(solution)/shard_map/dot_general | solution.py:40
  379.9 7.9 %fusion.56 = f32[1,512,128]{1,2,0:T(8,128)S(1)} fusion(f32[5120,128]{0,1:T(8,128)S(1)} %copy-done.2, bf16[4,512,5120]{2,1,0:T(8,128)(2,1)} %param.2), kind=kOutput, calls=%fused_computation.62 | convolution fusion | flops 4026531840 | bytes 8126464 | tf_op jit(solution)/shard_map/dot_general | solution.py:40
  387.8 13.8 %fusion.14 = f32[5120,128]{0,1:T(8,128)} fusion(bf16[4,512,5120]{2,1,0:T(8,128)(2,1)} %param.2, f32[5120,128]{0,1:T(8,128)S(1)} %copy-done.2, f32[5120]{0:T(1024)S(1)} %broadcast_multiply_fusion.1, f32[1,512,128]{1,2,0:T(8,128)S(1)} %fusion.83, f32[1,512,128]{1,2,0:T(8,128)S(1)} %fusion.74, f32[1,512,128]{1,2,0:T(8,128)S(1)} %fusion.65, ...), kind=kOutput, calls=%fused_computation.20 | convolution fusion | flops 16109535232 | bytes 27283456 | tf_op jit(solution)/shard_map/tnk,tnc->kc/dot_general | solution.py:50
  401.5 0.0 copy-start.3
  401.5 0.0 reduce-scatter.9.cloned.1.call-update
  401.5 0.0 all-gather.11.cloned.1.call-start
  401.6 69.6 %reduce-scatter.9.cloned.1.call-done = f32[640,128]{0,1:T(8,128)} async-done(((f32[5120,128]{0,1:T(8,128)}), f32[640,128]{0,1:T(8,128)}) %reduce-scatter.9.cloned.1.call-update) | async-done | bytes 327696 | tf_op jit(solution)/shard_map/reduce_scatter | solution.py:51
  471.2 0.0 copy-done.3
  471.2 1.1 multiply_reduce_fusion.3
  472.3 19.2 %all-reduce = (f32[128]{0:T(128)S(1)}, f32[128]{0:T(128)S(1)}) all-reduce(f32[128]{0:T(128)S(1)} %get-tuple-element.6, f32[128]{0:T(128)S(1)} %get-tuple-element.5), channel_id=1, replica_groups=mesh['dp'=8,'mp'=4] {'dp'}, use_global_device_ids=true, to_apply=%region_6.0 | all-reduce | flops 256 | bytes 2048 | tf_op jit(solution)/shard_map/psum | solution.py:59
  491.6 1.2 multiply_reduce_fusion.2
  492.7 17.2 %psum.30 = f32[128]{0:T(128)S(1)} all-reduce(f32[128]{0:T(128)S(1)} %multiply_reduce_fusion.2), channel_id=1, replica_groups=mesh['dp'=8,'mp'=4] {'dp'}, use_global_device_ids=true, to_apply=%region_11.0 | all-reduce | flops 128 | bytes 1024 | tf_op jit(solution)/shard_map/psum | solution.py:59
  509.9 1.8 multiply_add_fusion.1
  511.7 0.0 all-gather.11.cloned.1.call-update
  511.8 0.4 reduce-scatter.11.cloned.1.call-start
  512.2 52.9 %all-gather.11.cloned.1.call-done = f32[5120,128]{0,1:T(8,128)} async-done(((f32[640,128]{0,1:T(8,128)}), f32[5120,128]{0,1:T(8,128)}) %all-gather.11.cloned.1.call-update) | async-done | bytes 2621456 | tf_op jit(solution)/shard_map/all_gather | solution.py:37
  565.1 0.0 copy-start.1
  565.1 8.6 %fusion.86 = f32[1,512,128]{1,2,0:T(8,128)S(1)} fusion(f32[5120,128]{0,1:T(8,128)} %all-gather.11.cloned.1.call-done, bf16[4,512,5120]{2,1,0:T(8,128)(2,1)} %param.2), kind=kOutput, calls=%fused_computation.72 | convolution fusion | flops 4026531840 | bytes 8126464 | tf_op jit(solution)/shard_map/dot_general | solution.py:40
  573.8 0.0 copy-done.1
  573.8 7.7 %fusion.77 = f32[1,512,128]{1,2,0:T(8,128)S(1)} fusion(f32[5120,128]{0,1:T(8,128)S(1)} %copy-done.1, bf16[4,512,5120]{2,1,0:T(8,128)(2,1)} %param.2), kind=kOutput, calls=%fused_computation.69 | convolution fusion | flops 4026531840 | bytes 8126464 | tf_op jit(solution)/shard_map/dot_general | solution.py:40
  581.5 7.7 %fusion.68 = f32[1,512,128]{1,2,0:T(8,128)S(1)} fusion(f32[5120,128]{0,1:T(8,128)S(1)} %copy-done.1, bf16[4,512,5120]{2,1,0:T(8,128)(2,1)} %param.2), kind=kOutput, calls=%fused_computation.66 | convolution fusion | flops 4026531840 | bytes 8126464 | tf_op jit(solution)/shard_map/dot_general | solution.py:40
  589.2 7.9 %fusion.59 = f32[1,512,128]{1,2,0:T(8,128)S(1)} fusion(f32[5120,128]{0,1:T(8,128)S(1)} %copy-done.1, bf16[4,512,5120]{2,1,0:T(8,128)(2,1)} %param.2), kind=kOutput, calls=%fused_computation.63 | convolution fusion | flops 4026531840 | bytes 8126464 | tf_op jit(solution)/shard_map/dot_general | solution.py:40
  597.0 13.8 %fusion.16 = f32[5120,128]{0,1:T(8,128)} fusion(bf16[4,512,5120]{2,1,0:T(8,128)(2,1)} %param.2, f32[5120,128]{0,1:T(8,128)S(1)} %copy-done.1, f32[5120]{0:T(1024)S(1)} %broadcast_multiply_fusion.1, f32[1,512,128]{1,2,0:T(8,128)S(1)} %fusion.86, f32[1,512,128]{1,2,0:T(8,128)S(1)} %fusion.77, f32[1,512,128]{1,2,0:T(8,128)S(1)} %fusion.68, ...), kind=kOutput, calls=%fused_computation.22 | convolution fusion | flops 16109535232 | bytes 27283456 | tf_op jit(solution)/shard_map/tnk,tnc->kc/dot_general | solution.py:50
  610.8 0.0 reduce-scatter.11.cloned.1.call-update
  610.8 69.7 %reduce-scatter.11.cloned.1.call-done = f32[640,128]{0,1:T(8,128)} async-done(((f32[5120,128]{0,1:T(8,128)}), f32[640,128]{0,1:T(8,128)}) %reduce-scatter.11.cloned.1.call-update) | async-done | bytes 327696 | tf_op jit(solution)/shard_map/reduce_scatter | solution.py:51
  680.5 0.0 copy-done.4
  680.5 1.1 multiply_reduce_fusion.1
  681.6 19.2 %psum.31 = f32[128]{0:T(128)S(1)} all-reduce(f32[128]{0:T(128)S(1)} %multiply_reduce_fusion.1), channel_id=1, replica_groups=mesh['dp'=8,'mp'=4] {'dp'}, use_global_device_ids=true, to_apply=%region_14.0 | all-reduce | flops 128 | bytes 1024 | tf_op jit(solution)/shard_map/psum | solution.py:67
  700.9 0.1 multiply_add_fusion
  701.0 0.9 copy.6
  (7 shorter events, 0.1 us)
Async XLA Ops:
  6.5 60.3 %all-gather.7.cloned.1.call-start = ((), (), s32[]{:S(2)}) async-start(), calls=%async_computation.6 | async-start | bytes 2949120 | tf_op jit(solution)/shard_map/all_gather | solution.py:37
  8.7 144.8 %all-gather.5.cloned.1.call-start = ((), (), s32[]{:S(2)}) async-start(), calls=%async_computation.4 | async-start | bytes 5898240 | tf_op jit(solution)/shard_map/all_gather | solution.py:20
  9.4 217.0 %reduce-scatter.7.cloned.1.call-start = ((), (), s32[]{:S(2)}) async-start(), calls=%async_computation.7 | async-start | bytes 2949120 | tf_op jit(solution)/shard_map/reduce_scatter | solution.py:51
  66.9 8.6 %copy-start = (f32[5120,128]{0,1:T(8,128)S(1)}, f32[5120,128]{0,1:T(8,128)}, u32[]{:S(2)}) copy-start(f32[5120,128]{0,1:T(8,128)} %all-gather.7.cloned.1.call-done) | copy-start | bytes 7864324
  113.2 186.8 %reduce-scatter.5.cloned.1.call-start = ((), (), s32[]{:S(2)}) async-start(), calls=%async_computation.5 | async-start | bytes 2949120 | tf_op jit(solution)/shard_map/reduce_scatter | solution.py:31
  191.0 164.8 %all-gather.9.cloned.1.call-start = ((), (), s32[]{:S(2)}) async-start(), calls=%async_computation.8 | async-start | bytes 2949120 | tf_op jit(solution)/shard_map/all_gather | solution.py:37
  301.9 169.3 %reduce-scatter.9.cloned.1.call-start = ((), (), s32[]{:S(2)}) async-start(), calls=%async_computation.9 | async-start | bytes 2949120 | tf_op jit(solution)/shard_map/reduce_scatter | solution.py:51
  355.8 8.6 %copy-start.2 = (f32[5120,128]{0,1:T(8,128)S(1)}, f32[5120,128]{0,1:T(8,128)}, u32[]{:S(2)}) copy-start(f32[5120,128]{0,1:T(8,128)} %all-gather.9.cloned.1.call-done) | copy-start | bytes 7864324
  401.5 69.7 %copy-start.3 = (f32[640,128]{0,1:T(8,128)S(1)}, f32[640,128]{0,1:T(8,128)}, u32[]{:S(2)}) copy-start(f32[640,128]{0,1:T(8,128)} %sub.6) | copy-start | bytes 983044
  401.5 163.6 %all-gather.11.cloned.1.call-start = ((), (), s32[]{:S(2)}) async-start(), calls=%async_computation.10 | async-start | bytes 2949120 | tf_op jit(solution)/shard_map/all_gather | solution.py:37
  511.8 168.8 %reduce-scatter.11.cloned.1.call-start = ((), (), s32[]{:S(2)}) async-start(), calls=%async_computation.11 | async-start | bytes 2949120 | tf_op jit(solution)/shard_map/reduce_scatter | solution.py:51
  565.1 8.7 %copy-start.1 = (f32[5120,128]{0,1:T(8,128)S(1)}, f32[5120,128]{0,1:T(8,128)}, u32[]{:S(2)}) copy-start(f32[5120,128]{0,1:T(8,128)} %all-gather.11.cloned.1.call-done) | copy-start | bytes 7864324
  610.8 69.7 %copy-start.4 = (f32[640,128]{0,1:T(8,128)S(1)}, f32[640,128]{0,1:T(8,128)}, u32[]{:S(2)}) copy-start(f32[640,128]{0,1:T(8,128)} %multiply_add_fusion.1) | copy-start | bytes 983044
Sparse Core Ops, SparseCore 0:
  9.6 57.2 all-gather.6
  69.1 84.4 all-gather.4
  157.0 69.4 reduce-scatter.6
  229.8 70.1 reduce-scatter.4
  302.1 53.6 all-gather.8
  401.7 69.5 reduce-scatter.8
  511.9 53.1 all-gather.10
  610.9 69.5 reduce-scatter.10
where the time goes:
time: 719 us; the launch traced here: 709 us
  waiting for transfers between devices  444 us (62%)
  matrix products  162 us (23%)
  blocking collectives  55.6 us (8%)
  other arithmetic  28.6 us (4%)
  between operations  13.9 us (2%)
    reduce_scatter x3, waiting for transfers between devices, apply(): lax.psum_scatter((ALPHA * inner + (1.0 - ALPHA) * squares_all[:, None] *...  175 us
    all_gather x3, waiting for transfers between devices, apply(): full_vector = lax.all_gather(vector, 'dp', axis=0, tiled=True)  155 us
    dot_general x12, matrix products, apply(): jnp.dot(activations[task].astype(jnp.float32), full_vector, precision=lax...  96.2 us
    reduce_scatter x1, waiting for transfers between devices, shards(): lax.psum_scatter((ALPHA * cross + (1.0 - ALPHA) * diag_part) / total, 'dp...  73.5 us
    dot_general x3, matrix products, apply(): jnp.einsum('tnk,tnc->kc', rows_x, projected, precision=lax.Precision.HIGH...  41.3 us
    all_gather x1, waiting for transfers between devices, shards(): full_weights = lax.all_gather(task_weights, 'dp', axis=1, tiled=True)  40.3 us
    psum x2, blocking collectives, norm_of(): return lax.psum(column_sum(residual, residual), 'dp')  36.4 us
    dot_general x1, matrix products, shards(): jnp.einsum('tnk,tnc->kc', rows_x, outputs, preferred_element_type=jnp.flo...  24.7 us
  transfers between devices with their start and end apart: 8, of which 8 were waited for; matrix products, arithmetic and copies ran while one was open for 13% of the time, Pallas kernels for 0%

commit v1 on v0

v1 whole, which is shorter than its diff:
```python
import jax
import jax.numpy as jnp
from jax import lax
from jax.sharding import PartitionSpec as P

ALPHA = 0.9


def dot(left, right, dims):
    return lax.dot_general(
        left, right, (dims, ((), ())), preferred_element_type=jnp.float32
    )


def rounded(array):
    return lax.reduce_precision(array, 8, 7)


def split_pair(array):
    coarse = rounded(array)
    high = coarse.astype(jnp.bfloat16)
    low = (array - coarse).astype(jnp.bfloat16)
    return jnp.concatenate([high, low], axis=1)


def shards(activations, task_weights):
    tasks, tokens, width = activations.shape
    cols = task_weights.shape[2]
    total = tasks * tokens * lax.axis_size("dp")
    bf16, f32 = jnp.bfloat16, jnp.float32
    flat = activations.reshape(tasks * tokens, width)
    weights = lax.all_gather(task_weights, "dp", axis=1, tiled=True)
    squares = jnp.sum(jnp.square(activations.astype(f32)), axis=1)
    squares_all = jnp.sum(squares, axis=0)[:, None]
    mean = jnp.mean(weights.astype(f32), axis=0)
    mean_pair = split_pair(mean)
    gaps = []
    for task in range(tasks):
        wide = dot(
            activations[task],
            jnp.concatenate([weights[task], mean_pair], axis=1),
            ((1,), (0,)),
        )
        outputs = rounded(wide[:, :cols])
        gaps.append(outputs - (wide[:, cols : 2 * cols] + wide[:, 2 * cols :]))
    gap = split_pair(jnp.concatenate(gaps, axis=0))
    diag = sum(
        squares[t][:, None] * (weights[t].astype(f32) - mean) for t in range(tasks)
    )
    inner = dot(flat, gap, ((0,), (0,)))
    inner = inner[:, :cols] + inner[:, cols:]
    residual = lax.psum_scatter(
        (ALPHA * inner + (1.0 - ALPHA) * diag) / total,
        "dp",
        scatter_dimension=0,
        tiled=True,
    )
    full_bf = lax.all_gather(residual.astype(bf16), "dp", axis=0, tiled=True)
    full = full_bf.astype(f32)
    projected = split_pair(dot(flat, full_bf, ((1,), (0,))))
    inner = dot(flat, projected, ((0,), (0,)))
    inner = inner[:, :cols] + inner[:, cols:]
    image = lax.psum_scatter(
        (ALPHA * inner + (1.0 - ALPHA) * squares_all * full) / total,
        "dp",
        scatter_dimension=0,
        tiled=True,
    )
    image_full = lax.all_gather(image.astype(bf16), "dp", axis=0, tiled=True).astype(f32)
    norm0 = jnp.sum(full * full, axis=0)
    alpha0 = norm0 / jnp.sum(full * image_full, axis=0)
    next_full = full - alpha0 * image_full
    norm1 = jnp.sum(next_full * next_full, axis=0)
    beta = norm1 / norm0
    direction = next_full + beta * full
    direction_bf = direction.astype(bf16)
    direction = direction_bf.astype(f32)
    projected = dot(flat, direction_bf, ((1,), (0,)))
    energy = lax.psum(
        (
            ALPHA * jnp.sum(projected * projected, axis=0)
            + (1.0 - ALPHA) * jnp.sum(squares_all * direction * direction, axis=0)
        )
        / total,
        "dp",
    )
    alpha1 = norm1 / energy
    own_mean = jnp.mean(task_weights.astype(f32), axis=0)
    return (
        own_mean
        + alpha0 * residual
        + alpha1 * (residual - alpha0 * image + beta * residual)
    )


def solution(mesh):
    return jax.shard_map(
        shards,
        mesh=mesh,
        in_specs=(P(None, "dp", None), P(None, "dp", "mp")),
        out_specs=P("dp", "mp"),
        check_vma=False,
    )
```

time: 719 us -> 432 us (0.60); the launches traced: 709 us -> 432 us
  waiting for transfers between devices: 444 us -> 302 us
  matrix products: 162 us -> 58.9 us
  blocking collectives: 55.6 us -> 19 us
    reduce_scatter x4 -> x2, waiting for transfers between devices: 248 us -> 139 us  [the longest x1 69.6 us: shards(): lax.psum_scatter((ALPHA * inner + (1.0 - ALPHA) * diag) / total, 'dp', sc...]
    dot_general x16 -> x8, matrix products: 162 us -> 58.9 us  [dot(): lax.dot_general(left, right, (dims, ((), ())), preferred_element_type=jnp...]
    psum x3 -> x1, blocking collectives: 55.6 us -> 19 us  [shards(): lax.psum((ALPHA * jnp.sum(projected * projected, axis=0) + (1.0 - ALPHA)...]
    all_gather x4 -> x3, waiting for transfers between devices: 195 us -> 163 us  [the longest x1 79 us: shards(): weights = lax.all_gather(task_weights, 'dp', axis=1, tiled=True)]
    dot_general x1 -> x0, other arithmetic: 8.79 us -> none  [shards(): jnp.einsum('tnk,tnk->tk', activations, activations, preferred_element_typ...]
    div x4 -> x6, other arithmetic: 0.77 us -> 8.1 us  [the longest x1 6.02 us: shards(): (ALPHA * inner + (1.0 - ALPHA) * diag) / total]
  transfers between devices with their start and end apart: 8 -> 5, of which waited for: 8 -> 5; matrix products, arithmetic and copies ran while one was open for 13% -> 2% of each run, Pallas kernels for 0% -> 0%
where the time goes in v1:
time: 432 us
  waiting for transfers between devices  302 us (70%)
  matrix products  58.9 us (14%)
  other arithmetic  31.1 us (7%)
  blocking collectives  19 us (4%)
  between operations  13.3 us (3%)
  local copies, waits for them, and re-layouts  7.36 us (2%)
    all_gather x1, waiting for transfers between devices, shards(): weights = lax.all_gather(task_weights, 'dp', axis=1, tiled=True)  79 us
    reduce_scatter x1, waiting for transfers between devices, shards(): lax.psum_scatter((ALPHA * inner + (1.0 - ALPHA) * diag) / total, 'dp', sc...  69.6 us
    reduce_scatter x1, waiting for transfers between devices, shards(): lax.psum_scatter((ALPHA * inner + (1.0 - ALPHA) * squares_all * full) / t...  69.6 us
    dot_general x8, matrix products, dot(): lax.dot_general(left, right, (dims, ((), ())), preferred_element_type=jnp...  58.9 us
    all_gather x1, waiting for transfers between devices, shards(): full_bf = lax.all_gather(residual.astype(bf16), 'dp', axis=0, tiled=True)  42.2 us
    all_gather x1, waiting for transfers between devices, shards(): lax.all_gather(image.astype(bf16), 'dp', axis=0, tiled=True).astype(f32)  41.8 us
    psum x1, blocking collectives, shards(): lax.psum((ALPHA * jnp.sum(projected * projected, axis=0) + (1.0 - ALPHA)...  19 us
    reduce_sum x1, other arithmetic, shards(): squares_all = jnp.sum(squares, axis=0)[:, None]  9.47 us
  transfers between devices with their start and end apart: 5, of which 5 were waited for; matrix products, arithmetic and copies ran while one was open for 2% of the time, Pallas kernels for 0%

profile of v1, /device:TPU:0, one launch (start us, length us, event | category | flops | bytes accessed | tf_op | source)
XLA Modules:
  0.0 432.0 jit_solution(4052554290245626200)
XLA Ops:
  6.5 0.0 all-gather.4.cloned.1.call-start
  6.5 2.2 copy.6
  8.7 0.0 all-gather.4.cloned.1.call-update
  8.8 0.0 reduce-scatter.3.cloned.1.call-start
  8.8 9.5 %fusion = (f32[5120]{0:T(1024)S(1)}, f32[4,5120]{1,0:T(4,128)S(1)}) fusion(bf16[4,512,5120]{2,1,0:T(8,128)(2,1)} %param.2), kind=kLoop, calls=%fused_computation.1 | loop fusion | flops 41917440 | bytes 21073920 | tf_op jit(solution)/shard_map/reduce_sum | solution.py:34
  18.3 0.7 fusion.62
  18.9 79.0 %all-gather.4.cloned.1.call-done = bf16[4,5120,128]{1,2,0:T(8,128)(2,1)} async-done(((bf16[4,640,128]{1,2,0:T(8,128)(2,1)}), bf16[4,5120,128]{1,2,0:T(8,128)(2,1)}) %all-gather.4.cloned.1.call-update) | async-done | bytes 5242896 | tf_op jit(solution)/shard_map/all_gather | solution.py:32
  97.9 0.0 copy-start
  97.9 3.8 convert_reduce_fusion
  101.7 0.0 slice-start
  101.8 0.5 reduce-precision_convert_fusion
  102.2 0.0 copy-done
  102.2 0.0 slice-start.1
  102.3 0.0 slice-start.2
  102.3 2.1 slice_bitcast_fusion.3
  104.4 6.9 %fusion.30 = f32[512,384]{0,1:T(8,128)} fusion(bf16[4,512,5120]{2,1,0:T(8,128)(2,1)} %param.2, bf16[5120,128]{0,1:T(8,128)(2,1)S(1)} %get-tuple-element.16, bf16[5120,128]{0,1:T(8,128)(2,1)S(1)} %get-tuple-element.15, bf16[5120,128]{0,1:T(8,128)(2,1)} %get-tuple-element.11), kind=kOutput, calls=%fused_computation.65 | convolution fusion | flops 2025062400 | bytes 9961472 | tf_op jit(solution)/shard_map/dot_general | solution.py:10
  111.3 0.0 slice-done
  111.3 0.0 slice-done.1
  111.3 0.0 slice-done.2
  111.3 0.0 slice-done.3
  111.3 1.3 slice-done.4
  112.6 4.7 %fusion.33 = f32[512,384]{0,1:T(8,128)} fusion(bf16[4,512,5120]{2,1,0:T(8,128)(2,1)S(1)} %bitcast.65, bf16[5120,128]{0,1:T(8,128)(2,1)S(1)} %get-tuple-element.16, bf16[5120,128]{0,1:T(8,128)(2,1)S(1)} %get-tuple-element.15, bf16[5120,128]{0,1:T(8,128)(2,1)} %get-tuple-element.14), kind=kOutput, calls=%fused_computation.66 | convolution fusion | flops 2025062400 | bytes 9961472 | tf_op jit(solution)/shard_map/dot_general | solution.py:10
  117.2 3.7 fusion.36
  120.9 3.3 fusion.39
  124.2 1.6 fusion.53
  125.8 0.0 copy-done.6
  125.8 0.2 fusion.51
  126.0 0.2 reduce-precision_convert_fusion.2
  126.1 0.0 copy-start.7
  126.2 7.6 %convolution_bitcast_fusion.1 = f32[5120,256]{0,1:T(8,128)} fusion(bf16[2048,5120]{1,0:T(8,128)(2,1)S(1)} %bitcast.66, bf16[2048,128]{0,1:T(8,128)(2,1)S(1)} %get-tuple-element.20, bf16[2048,128]{0,1:T(8,128)(2,1)S(1)} %get-tuple-element.19), kind=kOutput, calls=%fused_computation.5 | convolution fusion | flops 5370806272 | bytes 27262976 | tf_op jit(solution)/shard_map/dot_general | solution.py:10
  133.8 0.0 copy-done.7
  133.8 6.0 %fusion.29 = f32[5120,128]{0,1:T(8,128)} fusion(f32[5120,256]{0,1:T(8,128)} %convolution_bitcast_fusion.1, f32[5120,128]{0,1:T(8,128)S(1)} %convert_reduce_fusion, f32[5120]{0:T(1024)S(1)} %bitcast.68, f32[5120]{0:T(1024)S(1)} %bitcast.69, f32[5120]{0:T(1024)S(1)} %bitcast.70, f32[5120]{0:T(1024)S(1)} %bitcast.67, ...), kind=kLoop, calls=%fused_computation.52 | loop fusion | flops 13762560 | bytes 15810560 | tf_op jit(solution)/shard_map/div | solution.py:53
  139.8 0.0 reduce-scatter.3.cloned.1.call-update
  139.8 0.0 all-gather.6.cloned.1.call-start
  139.9 69.6 %reduce-scatter.3.cloned.1.call-done = f32[640,128]{0,1:T(8,128)} async-done(((f32[5120,128]{0,1:T(8,128)}), f32[640,128]{0,1:T(8,128)}) %reduce-scatter.3.cloned.1.call-update) | async-done | bytes 327696 | tf_op jit(solution)/shard_map/reduce_scatter | solution.py:52
  209.4 1.7 convert_element_type.68
  211.1 0.0 all-gather.6.cloned.1.call-update
  211.1 0.0 reduce-scatter.5.cloned.1.call-start
  211.2 42.2 %all-gather.6.cloned.1.call-done = bf16[5120,128]{0,1:T(8,128)(2,1)} async-done(((bf16[640,128]{0,1:T(8,128)(2,1)}), bf16[5120,128]{0,1:T(8,128)(2,1)}) %all-gather.6.cloned.1.call-update) | async-done | bytes 1310736 | tf_op jit(solution)/shard_map/all_gather | solution.py:58
  253.4 11.6 %reduce-precision_convert_fusion.1 = (bf16[2048,128]{0,1:T(8,128)(2,1)S(1)}, bf16[2048,128]{0,1:T(8,128)(2,1)S(1)}) fusion(bf16[5120,128]{0,1:T(8,128)(2,1)} %all-gather.6.cloned.1.call-done, bf16[2048,5120]{1,0:T(8,128)(2,1)} %bitcast.61), kind=kOutput, calls=%fused_computation.57 | convolution fusion | flops 2685403136 | bytes 23330816 | tf_op jit(solution)/shard_map/dot_general | solution.py:10
  265.0 0.0 copy-start.1
  265.0 10.0 %convolution_bitcast_fusion = f32[5120,256]{0,1:T(8,128)S(1)} fusion(bf16[2048,5120]{1,0:T(8,128)(2,1)} %bitcast.62, bf16[2048,128]{0,1:T(8,128)(2,1)S(1)} %get-tuple-element.18, bf16[2048,128]{0,1:T(8,128)(2,1)S(1)} %get-tuple-element.17), kind=kOutput, calls=%fused_computation.4 | convolution fusion | flops 5370806272 | bytes 27262976 | tf_op jit(solution)/shard_map/dot_general | solution.py:10
  275.0 0.0 copy-done.1
  275.0 2.0 fusion.22
  277.0 0.0 reduce-scatter.5.cloned.1.call-update
  277.0 0.0 all-gather.8.cloned.1.call-start
  277.1 69.6 %reduce-scatter.5.cloned.1.call-done = f32[640,128]{0,1:T(8,128)} async-done(((f32[5120,128]{0,1:T(8,128)}), f32[640,128]{0,1:T(8,128)}) %reduce-scatter.5.cloned.1.call-update) | async-done | bytes 327696 | tf_op jit(solution)/shard_map/reduce_scatter | solution.py:63
  346.6 1.7 convert_element_type.72
  348.3 0.0 all-gather.8.cloned.1.call-update
  348.3 0.0 copy-done.3
  348.3 0.1 convert_reduce_fusion.1
  348.4 0.2 copy.5
  348.6 41.8 %all-gather.8.cloned.1.call-done = bf16[5120,128]{0,1:T(8,128)(2,1)} async-done(((bf16[640,128]{0,1:T(8,128)(2,1)}), bf16[5120,128]{0,1:T(8,128)(2,1)}) %all-gather.8.cloned.1.call-update) | async-done | bytes 1310736 | tf_op jit(solution)/shard_map/all_gather | solution.py:69
  390.4 2.0 fusion.23
  392.5 0.0 copy-done.2
  392.5 0.7 multiply_reduce_fusion
  393.1 1.1 fusion.19
  394.3 0.0 copy-start.5
  394.3 11.1 %fusion.42 = f32[128]{0:T(128)S(1)} fusion(bf16[5120,128]{0,1:T(8,128)(2,1)S(1)} %get-tuple-element.10, bf16[2048,5120]{1,0:T(8,128)(2,1)} %bitcast.63), kind=kOutput, calls=%fused_computation.69 | convolution fusion | flops 2684878848 | bytes 22282752 | tf_op jit(solution)/shard_map/dot_general | solution.py:10
  405.4 19.0 %psum.7 = f32[128]{0:T(128)S(1)} all-reduce(f32[128]{0:T(128)S(1)} %add_multiply_fusion), channel_id=1, replica_groups=mesh['dp'=8,'mp'=4] {'dp'}, use_global_device_ids=true, to_apply=%region_11.0 | all-reduce | flops 128 | bytes 1024 | tf_op jit(solution)/shard_map/psum | solution.py:79
  424.4 0.0 copy-done.4
  424.4 0.0 copy-done.5
  424.4 0.2 multiply_add_fusion
  424.6 0.9 copy.7
  (12 shorter events, 0.0 us)
Async XLA Ops:
  6.5 91.4 %all-gather.4.cloned.1.call-start = ((), (), s32[]{:S(2)}) async-start(), calls=%async_computation.2 | async-start | bytes 5898240 | tf_op jit(solution)/shard_map/all_gather | solution.py:32
  8.8 200.7 %reduce-scatter.3.cloned.1.call-start = ((), (), s32[]{:S(2)}) async-start(), calls=%async_computation.3 | async-start | bytes 2949120 | tf_op jit(solution)/shard_map/reduce_scatter | solution.py:52
  97.9 4.3 copy-start
  101.7 9.5 %slice-start = ((s8[20971520]{0:T(1024)(128)(4,1)}), s8[4194304]{0:T(1024)(128)(4,1)S(1)}, s32[]{:S(2)}) async-start(s8[20971520]{0:T(1024)(128)(4,1)} %bitcast.64), calls=%async_computation.7 | async-start | bytes 8388608
  102.2 9.0 %slice-start.1 = ((s8[20971520]{0:T(1024)(128)(4,1)}), s8[4194304]{0:T(1024)(128)(4,1)S(1)}, s32[]{:S(2)}) async-start(s8[20971520]{0:T(1024)(128)(4,1)} %bitcast.64), calls=%async_computation.8 | async-start | bytes 8388608
  102.3 9.0 %slice-start.2 = ((s8[20971520]{0:T(1024)(128)(4,1)}), s8[4194304]{0:T(1024)(128)(4,1)S(1)}, s32[]{:S(2)}) async-start(s8[20971520]{0:T(1024)(128)(4,1)} %bitcast.64), calls=%async_computation.9 | async-start | bytes 8388608
  104.4 6.9 %slice-start.3 = ((s8[20971520]{0:T(1024)(128)(4,1)}), s8[4194304]{0:T(1024)(128)(4,1)S(1)}, s32[]{:S(2)}) async-start(s8[20971520]{0:T(1024)(128)(4,1)} %bitcast.64), calls=%async_computation.10 | async-start | bytes 8388608
  104.4 8.2 %slice-start.4 = ((s8[20971520]{0:T(1024)(128)(4,1)}), s8[4194304]{0:T(1024)(128)(4,1)S(1)}, s32[]{:S(2)}) async-start(s8[20971520]{0:T(1024)(128)(4,1)} %bitcast.64), calls=%async_computation.11 | async-start | bytes 8388608
  124.2 1.6 copy-start.6
  126.1 7.6 %copy-start.7 = (f32[1,5120]{1,0:T(1,128)S(1)}, f32[1,5120]{1,0:T(1,128)}, u32[]{:S(2)}) copy-start(f32[1,5120]{1,0:T(1,128)} %get-tuple-element.24) | copy-start | bytes 61444
  139.8 113.5 %all-gather.6.cloned.1.call-start = ((), (), s32[]{:S(2)}) async-start(), calls=%async_computation.4 | async-start | bytes 1474560 | tf_op jit(solution)/shard_map/all_gather | solution.py:58
  211.1 135.5 %reduce-scatter.5.cloned.1.call-start = ((), (), s32[]{:S(2)}) async-start(), calls=%async_computation.5 | async-start | bytes 2949120 | tf_op jit(solution)/shard_map/reduce_scatter | solution.py:63
  265.0 10.0 %copy-start.1 = (bf16[5120,128]{0,1:T(8,128)(2,1)S(1)}, bf16[5120,128]{0,1:T(8,128)(2,1)}, u32[]{:S(2)}) copy-start(bf16[5120,128]{0,1:T(8,128)(2,1)} %all-gather.6.cloned.1.call-done) | copy-start | bytes 3932164
  277.0 71.3 %copy-start.3 = (bf16[4,640,128]{2,1,0:T(8,128)(2,1)S(1)}, bf16[4,640,128]{2,1,0:T(8,128)(2,1)}, u32[]{:S(2)}) copy-start(bf16[4,640,128]{2,1,0:T(8,128)(2,1)} %param.3) | copy-start | bytes 1966084
  277.0 113.4 %all-gather.8.cloned.1.call-start = ((), (), s32[]{:S(2)}) async-start(), calls=%async_computation.6 | async-start | bytes 1474560 | tf_op jit(solution)/shard_map/all_gather | solution.py:69
  390.4 2.0 copy-start.2
  394.3 30.2 %copy-start.4 = (f32[640,128]{0,1:T(8,128)S(1)}, f32[640,128]{0,1:T(8,128)}, u32[]{:S(2)}) copy-start(f32[640,128]{0,1:T(8,128)} %reduce-scatter.3.cloned.1.call-done) | copy-start | bytes 983044
  394.3 30.1 %copy-start.5 = (f32[640,128]{0,1:T(8,128)S(1)}, f32[640,128]{0,1:T(8,128)}, u32[]{:S(2)}) copy-start(f32[640,128]{0,1:T(8,128)} %reduce-scatter.5.cloned.1.call-done) | copy-start | bytes 983044
Sparse Core Ops, SparseCore 0:
  9.5 88.3 all-gather.3
  139.9 69.4 reduce-scatter.2
  211.7 41.6 all-gather.5
  277.2 69.4 reduce-scatter.4
  348.7 41.6 all-gather.7

commit v2 on v1

--- a/solution.py
+++ b/solution.py
@@ -1,9 +1,236 @@
+import functools
+
 import jax
 import jax.numpy as jnp
 from jax import lax
+from jax.experimental import pallas as pl
+from jax.experimental.pallas import tpu as pltpu
 from jax.sharding import PartitionSpec as P
 
 ALPHA = 0.9
+
+
+MESH = pl.DeviceIdType.MESH
+
+
+def inner_of(count):
+    inner = 1
+    for size in range(1, count + 1):
+        if count % size == 0 and size * size <= count:
+            inner = size
+    return inner
+
+
+def remote(source, target, send, receive, device):
+    return pltpu.make_async_remote_copy(
+        src_ref=source,
+        dst_ref=target,
+        send_sem=send,
+        recv_sem=receive,
+        device_id={"dp": device},
+        device_id_type=MESH,
+    )
+
+
+def greet(devices):
+    barrier = pltpu.get_barrier_semaphore()
+    for device in devices:
+        pl.semaphore_signal(
+            barrier, inc=1, device_id={"dp": device}, device_id_type=MESH
+        )
+    pl.semaphore_wait(barrier, len(devices))
+
+
+def places(count, inner):
+    outer = count // inner
+    me = lax.axis_index("dp")
+    mine_out, mine_in = me // inner, me % inner
+    near = [mine_out * inner + (mine_in + d) % inner for d in range(1, inner)]
+    far = [((mine_out + r) % outer) * inner + mine_in for r in range(1, outer)]
+    behind = [
+        ((mine_out - r + outer) % outer) * inner + mine_in for r in range(1, outer)
+    ]
+    return me, mine_out, mine_in, near, far, behind
+
+
+def reduce_gather_kernel(
+    count,
+    inner,
+    part_ref,
+    own_ref,
+    full_ref,
+    stage,
+    near_in,
+    sums,
+    far_in,
+    near_send,
+    near_recv,
+    far_send,
+    far_recv,
+    out_send,
+    out_recv,
+    spread_send,
+    spread_recv,
+):
+    outer = count // inner
+    me, mine_out, mine_in, near, far, behind = places(count, inner)
+    rows = own_ref.shape[0]
+    f32 = jnp.float32
+
+    def block(index):
+        return pl.ds(pl.multiple_of(index * rows, rows), rows)
+
+    greet(near + far)
+    order = list(range(1, outer)) + [0]
+    copies = {}
+    for r in order:
+        base = ((mine_out + r) % outer) * inner
+        for d in range(1, inner):
+            stage[r, d - 1] = part_ref[block(base + (mine_in + d) % inner)].astype(
+                stage.dtype
+            )
+            copies[r, d] = remote(
+                stage.at[r, d - 1],
+                near_in.at[r, d - 1],
+                near_send.at[r, d - 1],
+                near_recv.at[r, d - 1],
+                near[d - 1],
+            )
+            copies[r, d].start()
+    hops = []
+    for r in order:
+        base = ((mine_out + r) % outer) * inner
+        value = part_ref[block(base + mine_in)]
+        for d in range(1, inner):
+            copies[r, d].wait_recv()
+            value = value + near_in[r, d - 1].astype(f32)
+        if r:
+            sums[r - 1] = value.astype(sums.dtype)
+            hop = remote(
+                sums.at[r - 1],
+                far_in.at[r - 1],
+                far_send.at[r - 1],
+                far_recv.at[r - 1],
+                far[r - 1],
+            )
+            hop.start()
+            hops.append(hop)
+        else:
+            own_ref[...] = value
+    value = own_ref[...]
+    for r in range(1, outer):
+        hops[r - 1].wait_recv()
+        value = value + far_in[r - 1].astype(f32)
+    own_ref[...] = value
+    full_ref[block(me)] = value.astype(full_ref.dtype)
+
+    def spread(slot, index):
+        made = []
+        for d in range(1, inner):
+            copy = remote(
+                full_ref.at[block(index)],
+                full_ref.at[block(index)],
+                spread_send.at[slot, d - 1],
+                spread_recv.at[slot, d - 1],
+                near[d - 1],
+            )
+            copy.start()
+            made.append(copy)
+        return made
+
+    outs = []
+    for r in range(1, outer):
+        copy = remote(
+            full_ref.at[block(me)],
+            full_ref.at[block(me)],
+            out_send.at[r - 1],
+            out_recv.at[r - 1],
+            far[r - 1],
+        )
+        copy.start()
+        outs.append(copy)
+    spreads = spread(0, me)
+    for r in range(1, outer):
+        outs[r - 1].wait_recv()
+        spreads += spread(r, behind[r - 1])
+    for copy in spreads:
+        copy.wait_recv()
+    for copy in list(copies.values()) + hops + outs + spreads:
+        copy.wait_send()
+
+
+def reduce_gather(part, wire, collective_id):
+    count = lax.axis_size("dp")
+    inner = inner_of(count)
+    outer = count // inner
+    rows, cols = part.shape[0] // count, part.shape[1]
+    near, far = max(inner - 1, 1), max(outer - 1, 1)
+    dma = pltpu.SemaphoreType.DMA
+    vmem = pl.BlockSpec(memory_space=pltpu.VMEM)
+    return pl.pallas_call(
+        functools.partial(reduce_gather_kernel, count, inner),
+        out_shape=(
+            jax.ShapeDtypeStruct((rows, cols), jnp.float32),
+            jax.ShapeDtypeStruct((count * rows, cols), jnp.bfloat16),
+        ),
+        in_specs=[vmem],
+        out_specs=(vmem, vmem),
+        scratch_shapes=[
+            pltpu.VMEM((outer, near, rows, cols), wire),
+            pltpu.VMEM((outer, near, rows, cols), wire),
+            pltpu.VMEM((far, rows, cols), wire),
+            pltpu.VMEM((far, rows, cols), wire),
+            dma((outer, near)),
+            dma((outer, near)),
+            dma((far,)),
+            dma((far,)),
+            dma((far,)),
+            dma((far,)),
+            dma((outer, near)),
+            dma((outer, near)),
+        ],
+        compiler_params=pltpu.CompilerParams(
+            collective_id=collective_id, has_side_effects=True
+        ),
+    )(part)
+
+
+def total_kernel(count, in_ref, out_ref, slots, send, receive):
+    me = lax.axis_index("dp")
+    others = [(me + d) % count for d in range(1, count)]
+    greet(others)
+    copies = []
+    for d, device in enumerate(others):
+        copy = remote(in_ref, slots.at[d], send.at[d], receive.at[d], device)
+        copy.start()
+        copies.append(copy)
+    value = in_ref[...]
+    for d, copy in enumerate(copies):
+        copy.wait_recv()
+        value = value + slots[d]
+    out_ref[...] = value
+    for copy in copies:
+        copy.wait_send()
+
+
+def total_over(part, collective_id):
+    count = lax.axis_size("dp")
+    dma = pltpu.SemaphoreType.DMA
+    vmem = pl.BlockSpec(memory_space=pltpu.VMEM)
+    return pl.pallas_call(
+        functools.partial(total_kernel, count),
+        out_shape=jax.ShapeDtypeStruct(part.shape, jnp.float32),
+        in_specs=[vmem],
+        out_specs=vmem,
+        scratch_shapes=[
+            pltpu.VMEM((count - 1,) + part.shape, jnp.float32),
+            dma((count - 1,)),
+            dma((count - 1,)),
+        ],
+        compiler_params=pltpu.CompilerParams(
+            collective_id=collective_id, has_side_effects=True
+        ),
+    )(part)
 
 
 def dot(left, right, dims):
@@ -49,24 +276,17 @@
     )
     inner = dot(flat, gap, ((0,), (0,)))
     inner = inner[:, :cols] + inner[:, cols:]
-    residual = lax.psum_scatter(
-        (ALPHA * inner + (1.0 - ALPHA) * diag) / total,
-        "dp",
-        scatter_dimension=0,
-        tiled=True,
-    )
-    full_bf = lax.all_gather(residual.astype(bf16), "dp", axis=0, tiled=True)
+    residual, full_bf = reduce_gather(
+        (ALPHA * inner + (1.0 - ALPHA) * diag) / total, f32, 1
+    )
     full = full_bf.astype(f32)
     projected = split_pair(dot(flat, full_bf, ((1,), (0,))))
     inner = dot(flat, projected, ((0,), (0,)))
     inner = inner[:, :cols] + inner[:, cols:]
-    image = lax.psum_scatter(
-        (ALPHA * inner + (1.0 - ALPHA) * squares_all * full) / total,
-        "dp",
-        scatter_dimension=0,
-        tiled=True,
-    )
-    image_full = lax.all_gather(image.astype(bf16), "dp", axis=0, tiled=True).astype(f32)
+    image, image_bf = reduce_gather(
+        (ALPHA * inner + (1.0 - ALPHA) * squares_all * full) / total, bf16, 2
+    )
+    image_full = image_bf.astype(f32)
     norm0 = jnp.sum(full * full, axis=0)
     alpha0 = norm0 / jnp.sum(full * image_full, axis=0)
     next_full = full - alpha0 * image_full
@@ -76,14 +296,11 @@
     direction_bf = direction.astype(bf16)
     direction = direction_bf.astype(f32)
     projected = dot(flat, direction_bf, ((1,), (0,)))
-    energy = lax.psum(
-        (
-            ALPHA * jnp.sum(projected * projected, axis=0)
-            + (1.0 - ALPHA) * jnp.sum(squares_all * direction * direction, axis=0)
-        )
-        / total,
-        "dp",
-    )
+    energy = (
+        ALPHA * jnp.sum(projected * projected, axis=0)
+        + (1.0 - ALPHA) * jnp.sum(squares_all * direction * direction, axis=0)
+    ) / total
+    energy = total_over(jnp.broadcast_to(energy, (8, cols)), 3)[0]
     alpha1 = norm1 / energy
     own_mean = jnp.mean(task_weights.astype(f32), axis=0)
     return (

time: 432 us -> 325 us (0.75)
  waiting for transfers between devices: 302 us -> 79.7 us
  Pallas kernels: 0 us -> 123 us
  blocking collectives: 19 us -> 0 us
  matrix products: 58.9 us -> 66.6 us
  other arithmetic: 31.1 us -> 37.4 us
    reduce_scatter x2 -> x0, waiting for transfers between devices: 139 us -> none  [the longest x1 69.6 us: shards(): lax.psum_scatter((ALPHA * inner + (1.0 - ALPHA) * diag) / total, 'dp', sc...]
    pallas_call x0 -> x3, Pallas kernels: none -> 123 us  [the longest x2 111 us: reduce_gather(): pl.pallas_call(functools.partial(reduce_gather_kernel, count, inner), out...]
    all_gather x2 -> x0, waiting for transfers between devices: 84 us -> none  [the longest x1 42.2 us: shards(): full_bf = lax.all_gather(residual.astype(bf16), 'dp', axis=0, tiled=True)]
    psum x1 -> x0, blocking collectives: 19 us -> none  [shards(): lax.psum((ALPHA * jnp.sum(projected * projected, axis=0) + (1.0 - ALPHA)...]
    dot_general x8, matrix products: 58.9 us -> 66.6 us  [dot(): lax.dot_general(left, right, (dims, ((), ())), preferred_element_type=jnp...]
  transfers between devices with their start and end apart: 5 -> 1, of which waited for: 5 -> 1; matrix products, arithmetic and copies ran while one was open for 2% -> 4% of each run, Pallas kernels for 0% -> 0%
where the time goes in v2:
time: 325 us; the launch traced here: 324 us
  Pallas kernels  123 us (38%)
  waiting for transfers between devices  79.7 us (25%)
  matrix products  66.6 us (20%)
  other arithmetic  37.4 us (12%)
  between operations  13.6 us (4%)
  local copies, waits for them, and re-layouts  3.85 us (1%)
    pallas_call x2, Pallas kernels, reduce_gather(): pl.pallas_call(functools.partial(reduce_gather_kernel, count, inner), out...  111 us
    all_gather x1, waiting for transfers between devices, shards(): weights = lax.all_gather(task_weights, 'dp', axis=1, tiled=True)  79 us
    dot_general x8, matrix products, dot(): lax.dot_general(left, right, (dims, ((), ())), preferred_element_type=jnp...  66.6 us
    pallas_call x1, Pallas kernels, total_over(): pl.pallas_call(functools.partial(total_kernel, count), out_shape=jax.Shap...  12.3 us
    reduce_sum x1, other arithmetic, shards(): squares_all = jnp.sum(squares, axis=0)[:, None]  9.47 us
    div x1, other arithmetic, shards(): (ALPHA * inner + (1.0 - ALPHA) * diag) / total  9.13 us
  transfers between devices with their start and end apart: 1, of which 1 were waited for; matrix products, arithmetic and copies ran while one was open for 4% of the time, Pallas kernels for 0%

profile of v2, /device:TPU:0, one launch (start us, length us, event | category | flops | bytes accessed | tf_op | source)
XLA Modules:
  0.0 324.4 jit_solution(12498751532324674514)
XLA Ops:
  6.5 0.0 all-gather.2.cloned.1.call-start
  6.5 0.7 all-gather.2.cloned.1.call-update
  7.3 1.2 convert_reduce_fusion.1
  8.5 9.5 %fusion = (f32[5120]{0:T(1024)S(1)}, f32[4,5120]{1,0:T(4,128)S(1)}) fusion(bf16[4,512,5120]{2,1,0:T(8,128)(2,1)} %param.2), kind=kLoop, calls=%fused_computation.1 | loop fusion | flops 41917440 | bytes 21073920 | tf_op jit(solution)/shard_map/reduce_sum | solution.py:261
  17.9 0.6 broadcast_multiply_fusion
  18.6 0.7 fusion.63
  19.2 79.0 %all-gather.2.cloned.1.call-done = bf16[4,5120,128]{2,1,0:T(8,128)(2,1)} async-done(((bf16[4,640,128]{2,1,0:T(8,128)(2,1)}), bf16[4,5120,128]{2,1,0:T(8,128)(2,1)}) %all-gather.2.cloned.1.call-update) | async-done | bytes 5242896 | tf_op jit(solution)/shard_map/all_gather | solution.py:259
  98.2 0.0 copy-start
  98.2 3.7 %convert_reduce_fusion = f32[5120,128]{1,0:T(8,128)S(1)} fusion(bf16[4,5120,128]{2,1,0:T(8,128)(2,1)} %all-gather.2.cloned.1.call-done), kind=kLoop, calls=%fused_computation.3 | loop fusion | flops 4587520 | bytes 7864320 | tf_op jit(solution)/shard_map/reduce_sum | solution.py:262
  101.9 0.0 slice-start
  101.9 0.4 reduce-precision_convert_fusion
  102.3 0.0 copy-done
  102.4 0.0 slice-start.1
  102.4 0.0 slice-start.2
  102.4 1.4 slice_bitcast_fusion.3
  103.8 0.0 slice-start.3
  103.8 0.0 slice-start.4
  103.8 6.8 %fusion.30 = f32[512,384]{0,1:T(8,128)} fusion(bf16[4,512,5120]{2,1,0:T(8,128)(2,1)} %param.2, bf16[5120,128]{1,0:T(8,128)(2,1)S(1)} %get-tuple-element.22, bf16[5120,128]{1,0:T(8,128)(2,1)S(1)} %get-tuple-element.21, bf16[5120,128]{1,0:T(8,128)(2,1)} %get-tuple-element.17), kind=kOutput, calls=%fused_computation.65 | convolution fusion | flops 2025062400 | bytes 9961472 | tf_op jit(solution)/shard_map/dot_general | solution.py:237
  110.7 0.0 slice-done
  110.7 0.0 slice-done.1
  110.7 0.0 slice-done.2
  110.7 0.0 slice-done.3
  110.7 1.1 slice-done.4
  111.8 3.2 fusion.33
  114.9 2.2 fusion.36
  117.2 0.0 copy-start.3
  117.2 0.0 copy-start.4
  117.2 2.2 fusion.39
  119.5 0.0 copy-done.3
  119.5 0.0 copy-done.4
  119.5 0.2 fusion.53
  119.6 0.2 fusion.51
  119.8 1.0 reduce-precision_convert_fusion.2
  120.8 0.0 copy-start.7
  120.8 14.1 %convolution_bitcast_fusion.1 = f32[5120,256]{1,0:T(8,128)} fusion(bf16[2048,5120]{1,0:T(8,128)(2,1)} %bitcast.66, bf16[2048,128]{0,1:T(8,128)(2,1)} %get-tuple-element.26, bf16[2048,128]{0,1:T(8,128)(2,1)S(1)} %get-tuple-element.25), kind=kOutput, calls=%fused_computation.5 | convolution fusion | flops 5370806272 | bytes 27262976 | tf_op jit(solution)/shard_map/dot_general | solution.py:237
  134.9 0.0 copy-done.7
  134.9 9.1 %fusion.29.part_ref = f32[5120,128]{1,0:T(8,128)} fusion(f32[5120,256]{1,0:T(8,128)} %convolution_bitcast_fusion.1, f32[5120,128]{1,0:T(8,128)S(1)} %convert_reduce_fusion, f32[5120]{0:T(1024)S(1)} %bitcast.73, f32[5120]{0:T(1024)S(1)} %bitcast.74, f32[5120]{0:T(1024)S(1)} %bitcast.75, f32[5120]{0:T(1024)S(1)} %bitcast.72, ...), kind=kLoop, calls=%fused_computation.52 | loop fusion | flops 13762560 | bytes 15810560 | tf_op jit(solution)/shard_map/div | solution.py:280
  144.0 62.3 %shard_map.28 = (f32[640,128]{1,0:T(8,128)}, bf16[5120,128]{1,0:T(8,128)(2,1)}) custom-call(f32[5120,128]{1,0:T(8,128)} %fusion.29.part_ref), custom_call_target="tpu_custom_call" | custom-call | tf_op jit(solution)/shard_map/pallas_call | solution.py:170
  206.3 11.7 %reduce-precision_convert_fusion.1 = (bf16[2048,128]{0,1:T(8,128)(2,1)S(1)}, bf16[2048,128]{0,1:T(8,128)(2,1)S(1)}) fusion(bf16[5120,128]{1,0:T(8,128)(2,1)} %get-tuple-element.9, bf16[2048,5120]{1,0:T(8,128)(2,1)} %bitcast.67), kind=kOutput, calls=%fused_computation.57 | convolution fusion | flops 2685403136 | bytes 23330816 | tf_op jit(solution)/shard_map/dot_general | solution.py:237
  218.0 0.0 copy-start.1
  218.0 0.0 copy-start.8
  218.0 15.0 %convolution_bitcast_fusion = f32[5120,256]{1,0:T(8,128)} fusion(bf16[2048,5120]{1,0:T(8,128)(2,1)} %bitcast.68, bf16[2048,128]{0,1:T(8,128)(2,1)S(1)} %get-tuple-element.24, bf16[2048,128]{0,1:T(8,128)(2,1)S(1)} %get-tuple-element.23), kind=kOutput, calls=%fused_computation.4 | convolution fusion | flops 5370806272 | bytes 27262976 | tf_op jit(solution)/shard_map/dot_general | solution.py:237
  233.1 0.0 copy-done.1
  233.1 0.0 copy-done.8
  233.1 4.9 %fusion.22.part_ref = f32[5120,128]{1,0:T(8,128)} fusion(bf16[5120,128]{1,0:T(8,128)(2,1)S(1)} %copy-done.1, f32[5120,256]{1,0:T(8,128)} %convolution_bitcast_fusion, f32[5120]{0:T(1024)S(1)} %copy-done.8), kind=kLoop, calls=%fused_computation.43 | loop fusion | flops 3932160 | bytes 9195520 | tf_op jit(solution)/shard_map/div | solution.py:287
  238.0 48.7 %shard_map.29 = (f32[640,128]{1,0:T(8,128)}, bf16[5120,128]{1,0:T(8,128)(2,1)}) custom-call(f32[5120,128]{1,0:T(8,128)} %fusion.22.part_ref), custom_call_target="tpu_custom_call" | custom-call | tf_op jit(solution)/shard_map/pallas_call | solution.py:170
  286.7 0.0 copy-start.2
  286.7 2.1 fusion.23
  288.8 0.0 copy-done.2
  288.8 0.7 multiply_reduce_fusion
  289.6 11.3 %fusion.42 = f32[128]{0:T(128)S(1)} fusion(bf16[2048,5120]{1,0:T(8,128)(2,1)} %bitcast.69, bf16[5120,128]{1,0:T(8,128)(2,1)S(1)} %copy-done.1, bf16[5120,128]{1,0:T(8,128)(2,1)S(1)} %copy-done.2, f32[128]{0:T(128)S(1)} %div.49, f32[128]{0:T(128)S(1)} %div.48), kind=kOutput, calls=%fused_computation.69 | convolution fusion | flops 2689466368 | bytes 23594496 | tf_op jit(solution)/shard_map/dot_general | solution.py:237
  300.9 0.0 copy-start.5
  300.9 0.0 copy-start.6
  300.9 2.2 fusion.19
  303.1 0.6 broadcast_in_dim.2.in_ref
  303.7 12.3 %shard_map.30 = f32[8,128]{1,0:T(8,128)} custom-call(f32[8,128]{1,0:T(8,128)} %broadcast_in_dim.2.in_ref), custom_call_target="tpu_custom_call" | custom-call | tf_op jit(solution)/shard_map/pallas_call | solution.py:220
  316.1 0.7 fusion.56
  316.7 0.0 copy-done.5
  316.7 0.0 copy-done.6
  316.7 0.8 multiply_add_fusion
  (4 shorter events, 0.0 us)
Async XLA Ops:
  6.5 91.6 %all-gather.2.cloned.1.call-start = ((), (), s32[]{:S(2)}) async-start(), calls=%async_computation | async-start | bytes 5898240 | tf_op jit(solution)/shard_map/all_gather | solution.py:259
  98.2 4.2 %copy-start = (bf16[4,5120,128]{2,1,0:T(8,128)(2,1)S(1)}, bf16[4,5120,128]{2,1,0:T(8,128)(2,1)}, u32[]{:S(2)}) copy-start(bf16[4,5120,128]{2,1,0:T(8,128)(2,1)} %all-gather.2.cloned.1.call-done) | copy-start | bytes 15728644
  101.9 8.8 %slice-start = ((s8[20971520]{0:T(1024)(128)(4,1)}), s8[4194304]{0:T(1024)(128)(4,1)S(1)}, s32[]{:S(2)}) async-start(s8[20971520]{0:T(1024)(128)(4,1)} %bitcast.70), calls=%async_computation.1 | async-start | bytes 8388608
  102.4 8.3 %slice-start.1 = ((s8[20971520]{0:T(1024)(128)(4,1)}), s8[4194304]{0:T(1024)(128)(4,1)S(1)}, s32[]{:S(2)}) async-start(s8[20971520]{0:T(1024)(128)(4,1)} %bitcast.70), calls=%async_computation.2 | async-start | bytes 8388608
  102.4 8.3 %slice-start.2 = ((s8[20971520]{0:T(1024)(128)(4,1)}), s8[4194304]{0:T(1024)(128)(4,1)S(1)}, s32[]{:S(2)}) async-start(s8[20971520]{0:T(1024)(128)(4,1)} %bitcast.70), calls=%async_computation.3 | async-start | bytes 8388608
  103.8 6.8 %slice-start.3 = ((s8[20971520]{0:T(1024)(128)(4,1)}), s8[4194304]{0:T(1024)(128)(4,1)S(1)}, s32[]{:S(2)}) async-start(s8[20971520]{0:T(1024)(128)(4,1)} %bitcast.70), calls=%async_computation.4 | async-start | bytes 8388608
  103.8 7.9 %slice-start.4 = ((s8[20971520]{0:T(1024)(128)(4,1)}), s8[4194304]{0:T(1024)(128)(4,1)S(1)}, s32[]{:S(2)}) async-start(s8[20971520]{0:T(1024)(128)(4,1)} %bitcast.70), calls=%async_computation.5 | async-start | bytes 8388608
  117.2 2.3 copy-start.3
  117.2 2.3 copy-start.4
  120.8 14.1 %copy-start.7 = (f32[1,5120]{1,0:T(1,128)S(1)}, f32[1,5120]{1,0:T(1,128)}, u32[]{:S(2)}) copy-start(f32[1,5120]{1,0:T(1,128)} %get-tuple-element.30) | copy-start | bytes 61444
  218.0 15.0 %copy-start.1 = (bf16[5120,128]{1,0:T(8,128)(2,1)S(1)}, bf16[5120,128]{1,0:T(8,128)(2,1)}, u32[]{:S(2)}) copy-start(bf16[5120,128]{1,0:T(8,128)(2,1)} %get-tuple-element.9) | copy-start | bytes 3932164
  218.0 15.0 %copy-start.8 = (f32[5120]{0:T(1024)S(1)}, f32[5120]{0:T(1024)}, u32[]{:S(2)}) copy-start(f32[5120]{0:T(1024)} %broadcast_multiply_fusion) | copy-start | bytes 61444
  286.7 2.1 copy-start.2
  300.9 15.9 %copy-start.5 = (f32[640,128]{1,0:T(8,128)S(1)}, f32[640,128]{1,0:T(8,128)}, u32[]{:S(2)}) copy-start(f32[640,128]{1,0:T(8,128)} %get-tuple-element.11) | copy-start | bytes 983044
  300.9 15.9 %copy-start.6 = (f32[640,128]{1,0:T(8,128)S(1)}, f32[640,128]{1,0:T(8,128)}, u32[]{:S(2)}) copy-start(f32[640,128]{1,0:T(8,128)} %get-tuple-element.12) | copy-start | bytes 983044
Sparse Core Ops, SparseCore 0:
  9.5 88.6 all-gather.1

commit v3 on v2

--- a/solution.py
+++ b/solution.py
@@ -195,6 +195,124 @@
     )(part)
 
 
+def gather_kernel(
+    count,
+    inner,
+    wide,
+    in_ref,
+    x_ref,
+    full_ref,
+    squares_ref,
+    held,
+    load,
+    out_send,
+    out_recv,
+    spread_send,
+    spread_recv,
+):
+    outer = count // inner
+    me, mine_out, mine_in, near, far, behind = places(count, inner)
+    tasks, rows, _ = in_ref.shape
+    width = x_ref.shape[2]
+
+    def block(index):
+        return pl.ds(pl.multiple_of(index * rows, rows), rows)
+
+    def fetch(task):
+        return pltpu.make_async_copy(
+            x_ref.at[task], held.at[task % 2], load.at[task % 2]
+        )
+
+    fetch(0).start()
+    greet(near + far)
+    outs, spreads = {}, []
+    for task in range(tasks):
+        for r in range(1, outer):
+            outs[task, r] = remote(
+                in_ref.at[task],
+                full_ref.at[task, block(me)],
+                out_send.at[task, r - 1],
+                out_recv.at[task, r - 1],
+                far[r - 1],
+            )
+            outs[task, r].start()
+        for d in range(1, inner):
+            copy = remote(
+                in_ref.at[task],
+                full_ref.at[task, block(me)],
+                spread_send.at[task, 0, d - 1],
+                spread_recv.at[task, 0, d - 1],
+                near[d - 1],
+            )
+            copy.start()
+            spreads.append(copy)
+    for task in range(tasks):
+        full_ref[task, block(me)] = in_ref[task]
+    for task in range(tasks):
+        fetch(task).wait()
+        if task + 1 < tasks:
+            fetch(task + 1).start()
+
+        def body(step, carry, task=task):
+            span = pl.ds(pl.multiple_of(step * wide, wide), wide)
+            value = held[task % 2, :, span].astype(jnp.float32)
+            squares_ref[task, :, span] = jnp.sum(
+                value * value, axis=0, keepdims=True
+            )
+            return carry
+
+        lax.fori_loop(0, width // wide, body, 0)
+    for task in range(tasks):
+        for r in range(1, outer):
+            outs[task, r].wait_recv()
+            for d in range(1, inner):
+                copy = remote(
+                    full_ref.at[task, block(behind[r - 1])],
+                    full_ref.at[task, block(behind[r - 1])],
+                    spread_send.at[task, r, d - 1],
+                    spread_recv.at[task, r, d - 1],
+                    near[d - 1],
+                )
+                copy.start()
+                spreads.append(copy)
+    for copy in spreads:
+        copy.wait_recv()
+    for copy in list(outs.values()) + spreads:
+        copy.wait_send()
+
+
+def gather_weights(task_weights, activations, collective_id):
+    count = lax.axis_size("dp")
+    inner = inner_of(count)
+    outer = count // inner
+    tasks, rows, cols = task_weights.shape
+    _, tokens, width = activations.shape
+    near, far = max(inner - 1, 1), max(outer - 1, 1)
+    wide = 256 if width % 256 == 0 else width
+    dma = pltpu.SemaphoreType.DMA
+    vmem = pl.BlockSpec(memory_space=pltpu.VMEM)
+    return pl.pallas_call(
+        functools.partial(gather_kernel, count, inner, wide),
+        out_shape=(
+            jax.ShapeDtypeStruct((tasks, count * rows, cols), task_weights.dtype),
+            jax.ShapeDtypeStruct((tasks, 1, width), jnp.float32),
+        ),
+        in_specs=[vmem, pl.BlockSpec(memory_space=pl.ANY)],
+        out_specs=(vmem, vmem),
+        scratch_shapes=[
+            pltpu.VMEM((2, tokens, width), activations.dtype),
+            dma((2,)),
+            dma((tasks, far)),
+            dma((tasks, far)),
+            dma((tasks, outer, near)),
+            dma((tasks, outer, near)),
+        ],
+        compiler_params=pltpu.CompilerParams(
+            collective_id=collective_id, has_side_effects=True
+        ),
+    )(task_weights, activations)
+
+
 def total_kernel(count, in_ref, out_ref, slots, send, receive):
     me = lax.axis_index("dp")
     others = [(me + d) % count for d in range(1, count)]
@@ -256,8 +374,8 @@
     total = tasks * tokens * lax.axis_size("dp")
     bf16, f32 = jnp.bfloat16, jnp.float32
     flat = activations.reshape(tasks * tokens, width)
-    weights = lax.all_gather(task_weights, "dp", axis=1, tiled=True)
-    squares = jnp.sum(jnp.square(activations.astype(f32)), axis=1)
+    weights, squares = gather_weights(task_weights, activations, 4)
+    squares = squares.reshape(tasks, width)
     squares_all = jnp.sum(squares, axis=0)[:, None]
     mean = jnp.mean(weights.astype(f32), axis=0)
     mean_pair = split_pair(mean)

time: 325 us -> 296 us (0.911)
  waiting for transfers between devices: 79.7 us -> 0 us
  Pallas kernels: 123 us -> 199 us
  between operations: 13.6 us -> 0.19 us
  other arithmetic: 37.4 us -> 26.4 us
  matrix products: 66.6 us -> 62.9 us
    all_gather x1 -> x0, waiting for transfers between devices: 79 us -> none  [shards(): weights = lax.all_gather(task_weights, 'dp', axis=1, tiled=True)]
    pallas_call x0 -> x1, Pallas kernels: none -> 75.6 us  [gather_weights(): pl.pallas_call(functools.partial(gather_kernel, count, inner, wide), out_...]
    reduce_sum x1, other arithmetic: 9.47 us -> 0.08 us  [shards(): squares_all = jnp.sum(squares, axis=0)[:, None]]
    dot_general x8, matrix products: 66.6 us -> 62.9 us  [dot(): lax.dot_general(left, right, (dims, ((), ())), preferred_element_type=jnp...]
  transfers between devices with their start and end apart: 1 -> 0, of which waited for: 1 -> 0; matrix products, arithmetic and copies ran while one was open for 4% -> 0% of each run, Pallas kernels for 0% -> 0%
where the time goes in v3:
time: 296 us; the launch traced here: 295 us
  Pallas kernels  199 us (67%)
  matrix products  62.9 us (21%)
  other arithmetic  26.4 us (9%)
  local copies, waits for them, and re-layouts  6.62 us (2%)
    pallas_call x2, Pallas kernels, reduce_gather(): pl.pallas_call(functools.partial(reduce_gather_kernel, count, inner), out...  112 us
    pallas_call x1, Pallas kernels, gather_weights(): pl.pallas_call(functools.partial(gather_kernel, count, inner, wide), out_...  75.6 us
    dot_general x8, matrix products, dot(): lax.dot_general(left, right, (dims, ((), ())), preferred_element_type=jnp...  62.9 us
    pallas_call x1, Pallas kernels, total_over(): pl.pallas_call(functools.partial(total_kernel, count), out_shape=jax.Shap...  11.7 us
    div x1, other arithmetic, shards(): (ALPHA * inner + (1.0 - ALPHA) * diag) / total  9.14 us

profile of v3, /device:TPU:0, one launch (start us, length us, event | category | flops | bytes accessed | tf_op | source)
XLA Modules:
  0.0 295.5 jit_solution(9539394414591018859)
XLA Ops:
  0.0 75.6 %shard_map.28 = (bf16[4,5120,128]{2,1,0:T(8,128)(2,1)}, f32[4,1,5120]{2,1,0:T(1,128)}) custom-call(bf16[4,640,128]{2,1,0:T(8,128)(2,1)} %in_ref.1, bf16[4,512,5120]{2,1,0:T(8,128)(2,1)} %x_ref.1), custom_call_target="tpu_custom_call" | custom-call | tf_op jit(solution)/shard_map/pallas_call | solution.py:294
  75.6 0.0 copy-start
  75.6 3.6 %convert_reduce_fusion = f32[5120,128]{1,0:T(8,128)S(1)} fusion(bf16[4,5120,128]{2,1,0:T(8,128)(2,1)} %get-tuple-element.11), kind=kLoop, calls=%fused_computation | loop fusion | flops 4587520 | bytes 7864320 | tf_op jit(solution)/shard_map/reduce_sum | solution.py:380
  79.3 0.4 reduce-precision_convert_fusion
  79.7 3.6 %slice_bitcast_fusion.3 = (bf16[5120,128]{1,0:T(8,128)(2,1)S(1)}, bf16[5120,128]{1,0:T(8,128)(2,1)S(1)}, bf16[5120,128]{1,0:T(8,128)(2,1)S(1)}, bf16[5120,128]{1,0:T(8,128)(2,1)S(1)}) fusion(bf16[4,5120,128]{2,1,0:T(8,128)(2,1)} %get-tuple-element.11), kind=kLoop, calls=%fused_computation.60 | loop fusion | bytes 10485760 | tf_op jit(solution)/shard_map/squeeze | solution.py:386
  83.3 2.4 copy-done
  85.7 3.2 %fusion.28 = f32[512,384]{0,1:T(8,128)} fusion(bf16[4,512,5120]{2,1,0:T(8,128)(2,1)S(1)} %copy-done, bf16[5120,128]{1,0:T(8,128)(2,1)S(1)} %get-tuple-element.24, bf16[5120,128]{1,0:T(8,128)(2,1)S(1)} %get-tuple-element.23, bf16[5120,128]{1,0:T(8,128)(2,1)S(1)} %get-tuple-element.19), kind=kOutput, calls=%fused_computation.62 | convolution fusion | flops 2025062400 | bytes 9961472 | tf_op jit(solution)/shard_map/dot_general | solution.py:355
  88.9 0.0 copy-start.4
  88.9 2.3 fusion.31
  91.2 0.0 copy-done.4
  91.2 0.2 fusion.51
  91.3 2.3 fusion.34
  93.6 2.3 fusion.37
  95.9 0.2 fusion.49
  96.0 0.2 reduce-precision_convert_fusion.2
  96.2 0.0 copy-start.5
  96.2 14.9 %convolution_bitcast_fusion.1 = f32[5120,256]{1,0:T(8,128)} fusion(bf16[2048,5120]{1,0:T(8,128)(2,1)} %bitcast.66, bf16[2048,128]{0,1:T(8,128)(2,1)S(1)} %get-tuple-element.28, bf16[2048,128]{0,1:T(8,128)(2,1)S(1)} %get-tuple-element.27), kind=kOutput, calls=%fused_computation.2 | convolution fusion | flops 5370806272 | bytes 27262976 | tf_op jit(solution)/shard_map/dot_general | solution.py:355
  111.2 0.0 copy-done.5
  111.2 9.1 %fusion.27.part_ref = f32[5120,128]{1,0:T(8,128)} fusion(f32[5120,256]{1,0:T(8,128)} %convolution_bitcast_fusion.1, f32[5120,128]{1,0:T(8,128)S(1)} %convert_reduce_fusion, f32[5120]{0:T(1024)S(1)} %bitcast.71, f32[5120]{0:T(1024)S(1)} %bitcast.72, f32[5120]{0:T(1024)S(1)} %bitcast.73, f32[5120]{0:T(1024)S(1)} %bitcast.70, ...), kind=kLoop, calls=%fused_computation.49 | loop fusion | flops 13762560 | bytes 15810560 | tf_op jit(solution)/shard_map/div | solution.py:398
  120.3 65.2 %shard_map.29 = (f32[640,128]{1,0:T(8,128)}, bf16[5120,128]{1,0:T(8,128)(2,1)}) custom-call(f32[5120,128]{1,0:T(8,128)} %fusion.27.part_ref), custom_call_target="tpu_custom_call" | custom-call | tf_op jit(solution)/shard_map/pallas_call | solution.py:170
  185.5 11.7 %reduce-precision_convert_fusion.1 = (bf16[2048,128]{0,1:T(8,128)(2,1)S(1)}, bf16[2048,128]{0,1:T(8,128)(2,1)S(1)}) fusion(bf16[5120,128]{1,0:T(8,128)(2,1)} %get-tuple-element.13, bf16[2048,5120]{1,0:T(8,128)(2,1)} %bitcast.67), kind=kOutput, calls=%fused_computation.54 | convolution fusion | flops 2685403136 | bytes 23330816 | tf_op jit(solution)/shard_map/dot_general | solution.py:355
  197.2 0.0 copy-start.1
  197.2 15.0 %convolution_bitcast_fusion = f32[5120,256]{1,0:T(8,128)} fusion(bf16[2048,5120]{1,0:T(8,128)(2,1)} %bitcast.68, bf16[2048,128]{0,1:T(8,128)(2,1)S(1)} %get-tuple-element.26, bf16[2048,128]{0,1:T(8,128)(2,1)S(1)} %get-tuple-element.25), kind=kOutput, calls=%fused_computation.1 | convolution fusion | flops 5370806272 | bytes 27262976 | tf_op jit(solution)/shard_map/dot_general | solution.py:355
  212.2 0.1 reduce_sum.77
  212.3 0.0 copy-done.1
  212.3 4.9 %fusion.20.part_ref = f32[5120,128]{1,0:T(8,128)} fusion(bf16[5120,128]{1,0:T(8,128)(2,1)S(1)} %copy-done.1, f32[5120,256]{1,0:T(8,128)} %convolution_bitcast_fusion, f32[5120]{0:T(1024)S(1)} %broadcast_multiply_fusion), kind=kLoop, calls=%fused_computation.40 | loop fusion | flops 3932160 | bytes 9195520 | tf_op jit(solution)/shard_map/div | solution.py:405
  217.2 46.8 %shard_map.30 = (f32[640,128]{1,0:T(8,128)}, bf16[5120,128]{1,0:T(8,128)(2,1)}) custom-call(f32[5120,128]{1,0:T(8,128)} %fusion.20.part_ref), custom_call_target="tpu_custom_call" | custom-call | tf_op jit(solution)/shard_map/pallas_call | solution.py:170
  264.1 0.0 copy-start.2
  264.1 2.1 fusion.21
  266.2 0.0 copy-done.2
  266.2 0.7 multiply_reduce_fusion
  266.9 11.3 %fusion.40 = f32[128]{0:T(128)S(1)} fusion(bf16[2048,5120]{1,0:T(8,128)(2,1)} %bitcast.69, bf16[5120,128]{1,0:T(8,128)(2,1)S(1)} %copy-done.1, bf16[5120,128]{1,0:T(8,128)(2,1)S(1)} %copy-done.2, f32[128]{0:T(128)S(1)} %div.49, f32[128]{0:T(128)S(1)} %div.48), kind=kOutput, calls=%fused_computation.66 | convolution fusion | flops 2689466368 | bytes 23594496 | tf_op jit(solution)/shard_map/dot_general | solution.py:355
  278.2 0.0 copy-start.3
  278.2 2.2 fusion.17
  280.5 0.6 broadcast_in_dim.2.in_ref
  281.0 11.7 %shard_map.31 = f32[8,128]{1,0:T(8,128)} custom-call(f32[8,128]{1,0:T(8,128)} %broadcast_in_dim.2.in_ref), custom_call_target="tpu_custom_call" | custom-call | tf_op jit(solution)/shard_map/pallas_call | solution.py:338
  292.8 0.7 fusion.54
  293.5 0.0 copy-done.3
  293.5 0.1 convert_reduce_fusion.1
  293.6 1.9 multiply_add_fusion
  (5 shorter events, 0.0 us)
Async XLA Ops:
  75.6 10.1 %copy-start = (bf16[4,512,5120]{2,1,0:T(8,128)(2,1)S(1)}, bf16[4,512,5120]{2,1,0:T(8,128)(2,1)}, u32[]{:S(2)}) copy-start(bf16[4,512,5120]{2,1,0:T(8,128)(2,1)} %x_ref.1) | copy-start | bytes 62914564
  88.9 2.3 copy-start.4
  96.2 15.0 %copy-start.5 = (f32[4,1,5120]{2,1,0:T(1,128)S(1)}, f32[4,1,5120]{2,1,0:T(1,128)}, u32[]{:S(2)}) copy-start(f32[4,1,5120]{2,1,0:T(1,128)} %get-tuple-element.12) | copy-start | bytes 245764
  197.2 15.1 %copy-start.1 = (bf16[5120,128]{1,0:T(8,128)(2,1)S(1)}, bf16[5120,128]{1,0:T(8,128)(2,1)}, u32[]{:S(2)}) copy-start(bf16[5120,128]{1,0:T(8,128)(2,1)} %get-tuple-element.13) | copy-start | bytes 3932164
  264.1 2.1 copy-start.2
  278.2 15.3 %copy-start.3 = (bf16[4,640,128]{2,1,0:T(8,128)(2,1)S(1)}, bf16[4,640,128]{2,1,0:T(8,128)(2,1)}, u32[]{:S(2)}) copy-start(bf16[4,640,128]{2,1,0:T(8,128)(2,1)} %in_ref.1) | copy-start | bytes 1966084

commit v4 on v3

--- a/solution.py
+++ b/solution.py
@@ -398,9 +398,8 @@
         (ALPHA * inner + (1.0 - ALPHA) * diag) / total, f32, 1
     )
     full = full_bf.astype(f32)
-    projected = split_pair(dot(flat, full_bf, ((1,), (0,))))
+    projected = dot(flat, full_bf, ((1,), (0,))).astype(bf16)
     inner = dot(flat, projected, ((0,), (0,)))
-    inner = inner[:, :cols] + inner[:, cols:]
     image, image_bf = reduce_gather(
         (ALPHA * inner + (1.0 - ALPHA) * squares_all * full) / total, bf16, 2
     )

time: 296 us -> 293 us (0.990)
  other arithmetic: 26.4 us -> 21.6 us
    div x1 -> x0, other arithmetic: 4.94 us -> none  [shards(): (ALPHA * inner + (1.0 - ALPHA) * squares_all * full) / total]
    dot_general x8 -> x7, matrix products: 62.9 us -> 63.9 us  [dot(): lax.dot_general(left, right, (dims, ((), ())), preferred_element_type=jnp...]
where the time goes in v4:
time: 293 us; the launch traced here: 292 us
  Pallas kernels  199 us (68%)
  matrix products  63.9 us (22%)
  other arithmetic  21.6 us (7%)
  local copies, waits for them, and re-layouts  7.03 us (2%)
    pallas_call x2, Pallas kernels, reduce_gather(): pl.pallas_call(functools.partial(reduce_gather_kernel, count, inner), out...  112 us
    pallas_call x1, Pallas kernels, gather_weights(): pl.pallas_call(functools.partial(gather_kernel, count, inner, wide), out_...  75.6 us
    dot_general x7, matrix products, dot(): lax.dot_general(left, right, (dims, ((), ())), preferred_element_type=jnp...  63.9 us
    pallas_call x1, Pallas kernels, total_over(): pl.pallas_call(functools.partial(total_kernel, count), out_shape=jax.Shap...  11.7 us
    div x1, other arithmetic, shards(): (ALPHA * inner + (1.0 - ALPHA) * diag) / total  9.15 us

profile of v4, /device:TPU:0, one launch (start us, length us, event | category | flops | bytes accessed | tf_op | source)
XLA Modules:
  0.0 292.2 jit_solution(1202711245688202377)
XLA Ops:
  0.0 75.6 %shard_map.28 = (bf16[4,5120,128]{2,1,0:T(8,128)(2,1)}, f32[4,1,5120]{2,1,0:T(1,128)}) custom-call(bf16[4,640,128]{2,1,0:T(8,128)(2,1)} %in_ref.1, bf16[4,512,5120]{2,1,0:T(8,128)(2,1)} %x_ref.1), custom_call_target="tpu_custom_call" | custom-call | tf_op jit(solution)/shard_map/pallas_call | solution.py:294
  75.6 0.0 copy-start
  75.6 3.7 %convert_reduce_fusion = f32[5120,128]{1,0:T(8,128)S(1)} fusion(bf16[4,5120,128]{2,1,0:T(8,128)(2,1)} %get-tuple-element.11), kind=kLoop, calls=%fused_computation | loop fusion | flops 4587520 | bytes 7864320 | tf_op jit(solution)/shard_map/reduce_sum | solution.py:380
  79.4 0.4 reduce-precision_convert_fusion
  79.8 4.7 %slice_bitcast_fusion.3 = (bf16[5120,128]{1,0:T(8,128)(2,1)}, bf16[5120,128]{1,0:T(8,128)(2,1)S(1)}, bf16[5120,128]{1,0:T(8,128)(2,1)S(1)}, bf16[5120,128]{1,0:T(8,128)(2,1)S(1)}) fusion(bf16[4,5120,128]{2,1,0:T(8,128)(2,1)} %get-tuple-element.11), kind=kLoop, calls=%fused_computation.57 | loop fusion | bytes 10485760 | tf_op jit(solution)/shard_map/squeeze | solution.py:386
  84.5 1.7 copy-done
  86.2 3.6 %fusion.28 = f32[512,384]{0,1:T(8,128)S(1)} fusion(bf16[4,512,5120]{2,1,0:T(8,128)(2,1)S(1)} %copy-done, bf16[5120,128]{1,0:T(8,128)(2,1)S(1)} %get-tuple-element.24, bf16[5120,128]{1,0:T(8,128)(2,1)S(1)} %get-tuple-element.23, bf16[5120,128]{1,0:T(8,128)(2,1)} %get-tuple-element.19), kind=kOutput, calls=%fused_computation.59 | convolution fusion | flops 2025062400 | bytes 9961472 | tf_op jit(solution)/shard_map/dot_general | solution.py:355
  89.8 3.2 %fusion.31 = f32[512,384]{0,1:T(8,128)} fusion(bf16[4,512,5120]{2,1,0:T(8,128)(2,1)S(1)} %copy-done, bf16[5120,128]{1,0:T(8,128)(2,1)S(1)} %get-tuple-element.24, bf16[5120,128]{1,0:T(8,128)(2,1)S(1)} %get-tuple-element.23, bf16[5120,128]{1,0:T(8,128)(2,1)S(1)} %get-tuple-element.22), kind=kOutput, calls=%fused_computation.60 | convolution fusion | flops 2025062400 | bytes 9961472 | tf_op jit(solution)/shard_map/dot_general | solution.py:355
  93.0 1.3 fusion.47
  94.3 2.3 fusion.34
  96.5 2.3 fusion.37
  98.8 0.2 fusion.45
  99.0 0.2 reduce-precision_convert_fusion.1
  99.1 0.0 copy-start.4
  99.1 14.9 %convolution_bitcast_fusion = f32[5120,256]{1,0:T(8,128)} fusion(bf16[2048,5120]{1,0:T(8,128)(2,1)} %bitcast.68, bf16[2048,128]{0,1:T(8,128)(2,1)S(1)} %get-tuple-element.26, bf16[2048,128]{0,1:T(8,128)(2,1)S(1)} %get-tuple-element.25), kind=kOutput, calls=%fused_computation.1 | convolution fusion | flops 5370806272 | bytes 27262976 | tf_op jit(solution)/shard_map/dot_general | solution.py:355
  114.1 0.0 copy-done.4
  114.1 9.2 %fusion.27.part_ref = f32[5120,128]{1,0:T(8,128)} fusion(f32[5120,256]{1,0:T(8,128)} %convolution_bitcast_fusion, f32[5120,128]{1,0:T(8,128)S(1)} %convert_reduce_fusion, f32[5120]{0:T(1024)S(1)} %bitcast.72, f32[5120]{0:T(1024)S(1)} %bitcast.73, f32[5120]{0:T(1024)S(1)} %bitcast.74, f32[5120]{0:T(1024)S(1)} %bitcast.71, ...), kind=kLoop, calls=%fused_computation.48 | loop fusion | flops 13762560 | bytes 15810560 | tf_op jit(solution)/shard_map/div | solution.py:398
  123.2 65.2 %shard_map.29 = (f32[640,128]{1,0:T(8,128)}, bf16[5120,128]{1,0:T(8,128)(2,1)}) custom-call(f32[5120,128]{1,0:T(8,128)} %fusion.27.part_ref), custom_call_target="tpu_custom_call" | custom-call | tf_op jit(solution)/shard_map/pallas_call | solution.py:170
  188.4 0.1 reduce_sum.77
  188.5 26.2 %fusion.2.part_ref = f32[5120,128]{1,0:T(8,128)} fusion(bf16[2048,5120]{1,0:T(8,128)(2,1)} %bitcast.69, bf16[5120,128]{1,0:T(8,128)(2,1)} %get-tuple-element.13, f32[5120]{0:T(1024)S(1)} %broadcast_multiply_fusion), kind=kOutput, calls=%fused_computation.13 | convolution fusion | flops 5372248064 | bytes 24924160 | tf_op jit(solution)/shard_map/dot_general | solution.py:355
  214.7 0.0 copy-start.1
  214.7 46.9 %shard_map.30 = (f32[640,128]{1,0:T(8,128)}, bf16[5120,128]{1,0:T(8,128)(2,1)}) custom-call(f32[5120,128]{1,0:T(8,128)} %fusion.2.part_ref), custom_call_target="tpu_custom_call" | custom-call | tf_op jit(solution)/shard_map/pallas_call | solution.py:170
  261.6 0.0 copy-start.2
  261.6 0.0 copy-done.1
  261.6 2.1 fusion.22
  263.8 0.0 copy-done.2
  263.8 0.7 multiply_reduce_fusion
  264.5 11.5 %fusion.40 = f32[128]{0:T(128)S(1)} fusion(bf16[2048,5120]{1,0:T(8,128)(2,1)} %bitcast.70, bf16[5120,128]{1,0:T(8,128)(2,1)S(1)} %copy-done.1, bf16[5120,128]{1,0:T(8,128)(2,1)S(1)} %copy-done.2, f32[128]{0:T(128)S(1)} %div.49, f32[128]{0:T(128)S(1)} %div.48), kind=kOutput, calls=%fused_computation.63 | convolution fusion | flops 2689466368 | bytes 23594496 | tf_op jit(solution)/shard_map/dot_general | solution.py:355
  276.0 0.0 copy-start.3
  276.0 0.0 copy-start.5
  276.0 0.0 copy-start.6
  276.0 2.2 fusion.20
  278.3 0.6 broadcast_in_dim.2.in_ref
  278.9 11.7 %shard_map.31 = f32[8,128]{1,0:T(8,128)} custom-call(f32[8,128]{1,0:T(8,128)} %broadcast_in_dim.2.in_ref), custom_call_target="tpu_custom_call" | custom-call | tf_op jit(solution)/shard_map/pallas_call | solution.py:338
  290.6 0.7 fusion.50
  291.3 0.0 copy-done.3
  291.3 0.1 convert_reduce_fusion.1
  291.4 0.0 copy-done.5
  291.4 0.0 copy-done.6
  291.4 0.8 multiply_add_fusion
  (5 shorter events, 0.0 us)
Async XLA Ops:
  75.6 10.6 %copy-start = (bf16[4,512,5120]{2,1,0:T(8,128)(2,1)S(1)}, bf16[4,512,5120]{2,1,0:T(8,128)(2,1)}, u32[]{:S(2)}) copy-start(bf16[4,512,5120]{2,1,0:T(8,128)(2,1)} %x_ref.1) | copy-start | bytes 62914564
  99.1 15.0 %copy-start.4 = (f32[4,1,5120]{2,1,0:T(1,128)S(1)}, f32[4,1,5120]{2,1,0:T(1,128)}, u32[]{:S(2)}) copy-start(f32[4,1,5120]{2,1,0:T(1,128)} %get-tuple-element.12) | copy-start | bytes 245764
  214.7 46.9 %copy-start.1 = (bf16[5120,128]{1,0:T(8,128)(2,1)S(1)}, bf16[5120,128]{1,0:T(8,128)(2,1)}, u32[]{:S(2)}) copy-start(bf16[5120,128]{1,0:T(8,128)(2,1)} %get-tuple-element.13) | copy-start | bytes 3932164
  261.6 2.1 copy-start.2
  276.0 15.3 %copy-start.3 = (bf16[4,640,128]{2,1,0:T(8,128)(2,1)S(1)}, bf16[4,640,128]{2,1,0:T(8,128)(2,1)}, u32[]{:S(2)}) copy-start(bf16[4,640,128]{2,1,0:T(8,128)(2,1)} %in_ref.1) | copy-start | bytes 1966084
  276.0 15.3 %copy-start.5 = (f32[640,128]{1,0:T(8,128)S(1)}, f32[640,128]{1,0:T(8,128)}, u32[]{:S(2)}) copy-start(f32[640,128]{1,0:T(8,128)} %get-tuple-element.15) | copy-start | bytes 983044
  276.0 15.3 %copy-start.6 = (f32[640,128]{1,0:T(8,128)S(1)}, f32[640,128]{1,0:T(8,128)}, u32[]{:S(2)}) copy-start(f32[640,128]{1,0:T(8,128)} %get-tuple-element.16) | copy-start | bytes 983044
